TPU v7x, 32 devices: a whole 2x2x4 slice. The times are simulated.
32 devices in a mesh: seq: 16 (over z, x, core), tp: 2 (over y).
Axes of the slice: x: 2, y: 2, z: 4, core: 2. Of those that a mesh axis runs over, the one named last changes fastest.
Arguments:
- hidden: bfloat16 [8192, 4096], P('seq', 'tp'), may hold values from -6 to 6
- w_query: bfloat16 [4096, 4096], P(None, 'tp'), may hold values from -0.09375 to 0.09375
- w_key: bfloat16 [4096, 1024], P(None, 'tp'), may hold values from -0.09375 to 0.09375
- w_value: bfloat16 [4096, 1024], P(None, 'tp'), may hold values from -0.09375 to 0.09375
- w_out: bfloat16 [4096, 4096], P('tp'), may hold values from -0.09375 to 0.09375
- cache_keys: bfloat16 [256, 64, 1024], P('seq', None, 'tp'), may hold values from -52 to 52
- cache_values: bfloat16 [256, 64, 1024], P('seq', None, 'tp'), may hold values from -6 to 6
- cached_len: int32 [16], replicated, may hold values from 0 to 2048, as said below
- page_table: int32 [256, 2], P('seq'), may hold values from 0 to 31, as said below
Outputs:
- attn_out: bfloat16 [8192, 4096], P('seq', 'tp')
Inputs may be any that keep to these rules, and one draw needn't show every extreme that they name: `cached_len`: cached tokens of each request; some request has exactly 2048. `page_table`: row b is (r, j): pool block b holds request r's cached positions j * 64 to j * 64 + 63. Request r owns exactly ceil(cached_len[r] / 64) blocks, with places 0 to that count - 1, each once; every pool block is owned; the 16 blocks of one index of seq hold at most 2 blocks of any one request, and some index holds exactly 2 of some request.
All inputs are finite; a program needn't handle non-finite values.
Results may differ from a plain program's by a relative error of at most 0.019.
Values may be sent and summed in bfloat16 or wider, within the bound.
No kernel may reach another device: no remote copies, remote signals or barrier semaphores. Data moves between devices by JAX's collectives and lax.ppermute only.
A program may use at most 256 MiB of HBM per device.

v0:
```python
import math
import jax
import jax.numpy as jnp
from jax import lax
from jax.sharding import PartitionSpec as P

HD = 128
NEW = 512
CTX = 2048
ROPE_BASE = 1000000.0
masked_score = -1e30


def norm_rope(values, positions):
    values = values * lax.rsqrt(jnp.mean(values * values, axis=-1, keepdims=True) + 1e-06)
    half_width = values.shape[-1] // 2
    freqs = jnp.exp(
        jnp.arange(half_width, dtype=jnp.float32) * (-2.0 * math.log(ROPE_BASE) / values.shape[-1])
    )
    angles = positions.astype(jnp.float32)[:, None] * freqs[None, :]
    cosine = jnp.cos(angles)[:, None, :]
    sine = jnp.sin(angles)[:, None, :]
    first = values[..., :half_width]
    second = values[..., half_width:]
    return jnp.concatenate(
        [first * cosine - second * sine, second * cosine + first * sine], axis=-1
    )


def pick_rows(match, slot_count):
    ranking = jnp.cumsum(match.astype(jnp.int32)) - 1
    slot_ids = jnp.arange(slot_count, dtype=jnp.int32)
    chosen = match[None, :] & (ranking[None, :] == slot_ids[:, None])
    row_ids = jnp.arange(match.shape[0], dtype=jnp.int32)
    picked = jnp.sum(jnp.where(chosen, row_ids[None, :], 0), axis=1)
    present = jnp.any(chosen, axis=1)
    return (picked, present)


def on_device(
    hidden, w_query, w_key, w_value, w_out, cache_keys, cache_values, cached_len, page_table
):
    tokens_here = hidden.shape[0]
    query_heads = w_query.shape[1] // HD
    kv_heads = w_key.shape[1] // HD
    group = query_heads // kv_heads
    block_len = cache_keys.shape[1]
    width_kv = cache_keys.shape[2]
    span_count = NEW // tokens_here
    device = lax.axis_index("seq")
    request = device // span_count
    span = device % span_count
    length = cached_len[request]
    positions = length + span * tokens_here + jnp.arange(tokens_here, dtype=jnp.int32)
    piece = lax.all_gather(hidden, "tp", axis=1, tiled=True)

    def project(weight):
        return jnp.dot(piece, weight, preferred_element_type=jnp.float32)

    query_sum = project(w_query)
    key_sum = project(w_key)
    value_sum = project(w_value)
    queries = norm_rope(query_sum.reshape(tokens_here, query_heads, HD), positions).astype(
        jnp.bfloat16
    )
    grouped = (
        queries.reshape(tokens_here, kv_heads, group, HD)
        .transpose(1, 2, 0, 3)
        .reshape(kv_heads, group * tokens_here, HD)
    )
    fresh_keys = (
        norm_rope(key_sum.reshape(tokens_here, kv_heads, HD), positions)
        .astype(jnp.bfloat16)
        .reshape(tokens_here, kv_heads * HD)
    )
    fresh_values = value_sum.astype(jnp.bfloat16)
    row_query = span * tokens_here + jnp.arange(group * tokens_here, dtype=jnp.int32) % tokens_here

    def attend(state, keys, values, valid):
        keys = keys.reshape(-1, kv_heads, HD)
        values = values.reshape(-1, kv_heads, HD)
        scores = jnp.einsum(
            "krd,nkd->krn", grouped, keys, preferred_element_type=jnp.float32
        ) * HD ** (-0.5)
        scores = jnp.where(valid[None], scores, masked_score)
        running, total, accum = state
        newest = jnp.maximum(running, jnp.max(scores, axis=-1))
        weights = jnp.where(valid[None], jnp.exp(scores - newest[..., None]), 0.0)
        rescale = jnp.exp(running - newest)
        total = total * rescale + jnp.sum(weights, axis=-1)
        accum = accum * rescale[..., None] + jnp.einsum(
            "krn,nkd->krd", weights.astype(jnp.bfloat16), values, preferred_element_type=jnp.float32
        )
        return (newest, total, accum)

    state = (
        jnp.full((kv_heads, group * tokens_here), masked_score, jnp.float32),
        jnp.zeros((kv_heads, group * tokens_here), jnp.float32),
        jnp.zeros((kv_heads, group * tokens_here, HD), jnp.float32),
    )
    carry = state
    piece_keys = lax.all_gather(cache_keys[None], "seq", axis=0, tiled=True)
    piece_values = lax.all_gather(cache_values[None], "seq", axis=0, tiled=True)
    piece_table = lax.all_gather(page_table[None], "seq", axis=0, tiled=True)
    piece_fresh_k = lax.all_gather(fresh_keys[None], "seq", axis=0, tiled=True)
    piece_fresh_v = lax.all_gather(fresh_values[None], "seq", axis=0, tiled=True)
    source_count = piece_keys.shape[0]
    block_count = source_count * piece_keys.shape[1]
    per_peer = max(1, CTX // block_len // lax.axis_size("seq"))
    slot_count = min(block_count, source_count * per_peer)
    flat_table = piece_table.reshape(block_count, 2)
    places = flat_table[:, 1]
    match = (flat_table[:, 0] == request) & (places * block_len < length)
    picked, present = pick_rows(match, slot_count)
    keys_taken = piece_keys.reshape(block_count, block_len, width_kv)[picked].reshape(
        slot_count * block_len, width_kv
    )
    values_taken = piece_values.reshape(block_count, block_len, width_kv)[picked].reshape(
        slot_count * block_len, width_kv
    )
    key_pos = places[picked][:, None] * block_len + jnp.arange(block_len, dtype=jnp.int32)[None, :]
    valid = (present[:, None] & (key_pos < length)).reshape(1, slot_count * block_len)
    carry = attend(carry, keys_taken, values_taken, valid)
    sources = jnp.arange(source_count, dtype=jnp.int32)
    source_count = sources.shape[0]
    slot_count = min(source_count, span_count)
    match = (sources // span_count == request) & (sources % span_count <= span)
    picked, present = pick_rows(match, slot_count)
    keys_taken = piece_fresh_k[picked].reshape(slot_count * tokens_here, width_kv)
    values_taken = piece_fresh_v[picked].reshape(slot_count * tokens_here, width_kv)
    key_index = (sources[picked] % span_count)[:, None] * tokens_here + jnp.arange(
        tokens_here, dtype=jnp.int32
    )[None, :]
    live = jnp.broadcast_to(present[:, None], key_index.shape).reshape(-1)
    valid = live[None, :] & (key_index.reshape(-1)[None, :] <= row_query[:, None])
    state = attend(carry, keys_taken, values_taken, valid)
    running, total, accum = state
    attended = (accum / total[..., None]).astype(jnp.bfloat16)
    attended = (
        attended.reshape(kv_heads, group, tokens_here, HD)
        .transpose(2, 0, 1, 3)
        .reshape(tokens_here, query_heads * HD)
    )
    partial_out = jnp.dot(attended, w_out, preferred_element_type=jnp.float32)
    return lax.psum_scatter(partial_out.astype(jnp.bfloat16), "tp", scatter_dimension=1, tiled=True)


def solution(mesh):
    in_specs = (
        P("seq", "tp"),
        P(None, "tp"),
        P(None, "tp"),
        P(None, "tp"),
        P("tp", None),
        P("seq", None, "tp"),
        P("seq", None, "tp"),
        P(),
        P("seq", None),
    )
    out_specs = P("seq", "tp")
    return jax.shard_map(
        on_device, mesh=mesh, in_specs=in_specs, out_specs=out_specs, check_vma=False
    )
```

profile of v0, /device:TPU:0, one launch (start us, length us, event | category | flops | bytes accessed | tf_op | source)
XLA Modules:
  0.0 617.4 jit_solution(7555049823054470965)
XLA Ops:
  9.8 58.6 %all-gather.11.cloned.1.call-done = bf16[512,4096]{1,0:T(8,128)(2,1)} async-done(((bf16[512,2048]{1,0:T(8,128)(2,1)}), bf16[512,4096]{1,0:T(8,128)(2,1)}) %all-gather.11.cloned.1.call-update) | async-done | bytes 4194320 | tf_op jit(solution)/shard_map/all_gather | solution.py:55
  68.4 5.9 multiply_reduce_fusion.1
  75.7 6.6 %convolution_convert_fusion.1 = bf16[512,512]{1,0:T(8,128)(2,1)} fusion(bf16[512,4096]{1,0:T(8,128)(2,1)} %all-gather.11.cloned.1.call-done, bf16[4096,512]{1,0:T(8,128)(2,1)} %param.12), kind=kOutput, calls=%fused_computation.30 | convolution fusion | flops 2147745792 | bytes 8912896 | tf_op jit(solution)/shard_map/dot_general | solution.py:58
  83.8 21.8 %all-gather.4 = s32[16,16,2]{1,2,0:T(2,128)S(1)} all-gather(s32[1,16,2]{1,2,0:T(2,128)S(1)} %bitcast.60), channel_id=2, replica_groups=mesh['seq'=16,'tp'=2] {'seq'}, dimensions={0}, use_global_device_ids=true | all-gather | bytes 2176 | tf_op jit(solution)/shard_map/all_gather | solution.py:104
  113.9 12.9 %convolution_bitcast_fusion = f32[64,8,16,128]{3,1,2,0:T(8,128)S(1)} fusion(bf16[512,4096]{1,0:T(8,128)(2,1)} %all-gather.11.cloned.1.call-done, bf16[4096,2048]{1,0:T(8,128)(2,1)} %param.10), kind=kOutput, calls=%fused_computation.24 | convolution fusion | flops 8589934592 | bytes 25165824 | tf_op jit(solution)/shard_map/dot_general | solution.py:58
  131.3 4.1 broadcast_multiply_fusion
  139.2 11.7 %all-gather.13.cloned.1.call-done = bf16[16,512,512]{2,1,0:T(8,128)(2,1)} async-done(((bf16[1,512,512]{2,1,0:T(8,128)(2,1)}), bf16[16,512,512]{2,1,0:T(8,128)(2,1)}) %all-gather.13.cloned.1.call-update) | async-done | bytes 8388624 | tf_op jit(solution)/shard_map/all_gather | solution.py:105
  150.8 75.4 %all-gather.19.cloned.1.call-done = bf16[8192,512]{1,0:T(8,128)(2,1)} async-done(((bf16[512,512]{1,0:T(8,128)(2,1)}), bf16[8192,512]{1,0:T(8,128)(2,1)}) %all-gather.19.cloned.1.call-update) | async-done | bytes 8388624 | tf_op jit(solution)/shard_map/all_gather | solution.py:106
  226.2 2.2 constant_dynamic-slice_fusion
  230.5 2.1 copy.100
  232.6 8.5 %fusion.6 = (f32[4,2048]{1,0:T(4,128)S(1)}, f32[4,2048,512]{1,2,0:T(8,128)}) fusion(pred[2048,512]{0,1:T(8,128)(4,1)S(1)} %fusion.12, bf16[4,2048,128]{2,1,0:T(8,128)(2,1)S(1)} %bitcast.49, bf16[512,4,128]{0,2,1:T(8,128)(2,1)} %bitcast.53), kind=kOutput, calls=%fused_computation.12 | convolution fusion | flops 1086316544 | bytes 20480000 | tf_op jit(solution)/shard_map/krd,nkd->krn/dot_general | solution.py:82
  241.1 112.3 %all-gather.15.cloned.1.call-done = bf16[256,64,512]{2,1,0:T(8,128)(2,1)} async-done(((bf16[16,64,512]{2,1,0:T(8,128)(2,1)}), bf16[256,64,512]{2,1,0:T(8,128)(2,1)}) %all-gather.15.cloned.1.call-update) | async-done | bytes 16777232 | tf_op jit(solution)/shard_map/all_gather | solution.py:102
  353.4 7.8 %gather_fusion.1 = bf16[32,64,512]{2,1,0:T(8,128)(2,1)} fusion(bf16[256,64,512]{2,1,0:T(8,128)(2,1)} %all-gather.15.cloned.1.call-done, s32[1024]{0:T(1024)S(1)} %pad_clamp_fusion), kind=kCustom, calls=%fused_computation.1 | custom fusion | bytes 4194432 | tf_op jit(solution)/shard_map/gather | solution.py:115
  361.2 4.1 reshape_reshape.12
  365.3 25.8 %fusion = (f32[4,2048]{1,0:T(4,128)S(1)}, f32[4,2048,2048]{1,2,0:T(8,128)}) fusion(pred[2048]{0:T(1024)(128)(4,1)S(1)} %and.107, bf16[4,2048,128]{2,1,0:T(8,128)(2,1)S(1)} %bitcast.50, bf16[2048,4,128]{2,1,0:T(4,128)(2,1)} %reshape_reshape.12), kind=kOutput, calls=%fused_computation.5 | convolution fusion | flops 4345290752 | bytes 71337984 | tf_op jit(solution)/shard_map/krd,nkd->krn/dot_general | solution.py:82
  391.1 8.1 %fusion.7 = f32[4,2048]{1,0:T(4,128)S(1)} fusion(f32[4,2048,512]{1,2,0:T(8,128)} %get-tuple-element.45, f32[4,2048]{1,0:T(4,128)S(1)} %get-tuple-element.34, pred[2048,512]{0,1:T(8,128)(4,1)S(1)} %fusion.12), kind=kLoop, calls=%fused_computation.13 | loop fusion | flops 20963328 | bytes 17891328 | tf_op jit(solution)/shard_map/reduce_sum | solution.py:90
  399.2 10.6 %fusion.9 = f32[4,2048,128]{2,1,0:T(8,128)} fusion(bf16[512,4,128]{0,2,1:T(8,128)(2,1)S(1)} %bitcast.57, f32[4,2048,512]{1,2,0:T(8,128)} %get-tuple-element.45, f32[4,2048]{1,0:T(4,128)S(1)} %get-tuple-element.34, pred[2048,512]{0,1:T(8,128)(4,1)S(1)} %fusion.12), kind=kOutput, calls=%fused_computation.15 | convolution fusion | flops 1094713344 | bytes 22577152 | tf_op jit(solution)/shard_map/krn,nkd->krd/dot_general | solution.py:91
  409.8 70.7 %all-gather.17.cloned.1.call-done = bf16[256,64,512]{2,1,0:T(8,128)(2,1)} async-done(((bf16[16,64,512]{2,1,0:T(8,128)(2,1)}), bf16[256,64,512]{2,1,0:T(8,128)(2,1)}) %all-gather.17.cloned.1.call-update) | async-done | bytes 16777232 | tf_op jit(solution)/shard_map/all_gather | solution.py:103
  480.5 6.4 %gather_fusion.2 = bf16[32,64,512]{2,1,0:T(8,128)(2,1)S(1)} fusion(bf16[256,64,512]{2,1,0:T(8,128)(2,1)} %all-gather.17.cloned.1.call-done, s32[1024]{0:T(1024)S(1)} %pad_clamp_fusion), kind=kCustom, calls=%fused_computation.2 | custom fusion | bytes 4194432 | tf_op jit(solution)/shard_map/gather | solution.py:118
  489.0 21.6 %fusion.1 = f32[4,2048]{1,0:T(4,128)S(1)} fusion(f32[4,2048,2048]{1,2,0:T(8,128)} %get-tuple-element.43, f32[4,2048]{1,0:T(4,128)S(1)} %get-tuple-element.35, pred[2048]{0:T(1024)(128)(4,1)S(1)} %and.107), kind=kLoop, calls=%fused_computation.6 | loop fusion | flops 83877888 | bytes 67176448 | tf_op jit(solution)/shard_map/reduce_sum | solution.py:90
  510.7 30.3 %divide_convert_fusion = bf16[4,2048,128]{2,1,0:T(8,128)(2,1)} fusion(f32[4,2048,128]{2,1,0:T(8,128)} %fusion.9, f32[4,2048,2048]{1,2,0:T(8,128)} %get-tuple-element.43, f32[4,2048]{1,0:T(4,128)S(1)} %get-tuple-element.35, pred[2048]{0:T(1024)(128)(4,1)S(1)} %and.107, bf16[2048,4,128]{2,1,0:T(4,128)(2,1)S(1)} %copy-done.1, ...), kind=kOutput, calls=%fused_computation.18 | convolution fusion | flops 4384096256 | bytes 75630592 | tf_op jit(solution)/shard_map/krn,nkd->krd/dot_general | solution.py:91
  541.0 2.8 copy.93
  543.8 13.9 %convolution_convert_fusion = bf16[512,4096]{1,0:T(8,128)(2,1)} fusion(bf16[512,2048]{0,1:T(8,128)(2,1)S(1)} %bitcast.55, bf16[2048,4096]{1,0:T(8,128)(2,1)} %param.13), kind=kOutput, calls=%fused_computation.17 | convolution fusion | flops 8592031744 | bytes 23068672 | tf_op jit(solution)/shard_map/dot_general | solution.py:144
  557.7 52.6 %reduce-scatter.2.cloned.1.call-done = bf16[512,2048]{1,0:T(8,128)(2,1)} async-done(((bf16[512,4096]{1,0:T(8,128)(2,1)}), bf16[512,2048]{1,0:T(8,128)(2,1)}) %reduce-scatter.2.cloned.1.call-update) | async-done | bytes 2097168 | tf_op jit(solution)/shard_map/reduce_scatter | solution.py:145
  (69 shorter events, 24.9 us)
Async XLA Ops:
  6.5 61.8 %all-gather.11.cloned.1.call-start = ((), (), s32[]{:S(2)}) async-start(), calls=%async_computation.1 | async-start | bytes 6291456 | tf_op jit(solution)/shard_map/all_gather | solution.py:55
  7.3 143.6 %all-gather.13.cloned.1.call-start = ((), (), s32[]{:S(2)}) async-start(), calls=%async_computation.2 | async-start | bytes 8912896 | tf_op jit(solution)/shard_map/all_gather | solution.py:105
  75.7 8.2 %copy-start.3 = (s32[16,2]{0,1:T(2,128)S(1)}, s32[16,2]{0,1:T(2,128)}, u32[]{:S(2)}) copy-start(s32[16,2]{0,1:T(2,128)} %param.17) | copy-start | bytes 388
  75.7 150.5 %all-gather.19.cloned.1.call-start = ((), (), s32[]{:S(2)}) async-start(), calls=%async_computation.6 | async-start | bytes 8912896 | tf_op jit(solution)/shard_map/all_gather | solution.py:106
  82.3 271.1 %all-gather.15.cloned.1.call-start = ((), (), s32[]{:S(2)}) async-start(), calls=%async_computation.4 | async-start | bytes 17825792 | tf_op jit(solution)/shard_map/all_gather | solution.py:102
  82.9 397.6 %all-gather.17.cloned.1.call-start = ((), (), s32[]{:S(2)}) async-start(), calls=%async_computation.5 | async-start | bytes 17825792 | tf_op jit(solution)/shard_map/all_gather | solution.py:103
  83.5 526.8 %reduce-scatter.2.cloned.1.call-start = ((), (), s32[]{:S(2)}) async-start(), calls=%async_computation.3 | async-start | bytes 6291456 | tf_op jit(solution)/shard_map/reduce_scatter | solution.py:145
  127.8 2.0 copy-start
  391.1 8.1 %copy-start.2 = (bf16[1,512,512]{1,2,0:T(8,128)(2,1)S(1)}, bf16[1,512,512]{1,2,0:T(8,128)(2,1)}, u32[]{:S(2)}) copy-start(bf16[1,512,512]{1,2,0:T(8,128)(2,1)} %copy.100) | copy-start | bytes 1572868
  489.0 21.7 %copy-start.1 = (bf16[2048,4,128]{2,1,0:T(4,128)(2,1)S(1)}, bf16[2048,4,128]{2,1,0:T(4,128)(2,1)}, u32[]{:S(2)}) copy-start(bf16[2048,4,128]{2,1,0:T(4,128)(2,1)} %reshape_reshape.13) | copy-start | bytes 6291460
Sparse Core Ops, SparseCore 0:
  8.9 59.4 all-gather.10
  75.8 75.0 all-gather.12
  153.0 73.1 all-gather.18
  228.2 125.1 all-gather.14
  355.4 125.0 all-gather.16
  557.8 52.4 reduce-scatter.1
where the time goes:
time: 622 us; the launch traced here: 617 us
  waiting for transfers between devices  383 us (62%)
  matrix products  114 us (18%)
  other arithmetic  44.7 us (7%)
  local copies, waits for them, and re-layouts  37.4 us (6%)
  blocking collectives  21.8 us (4%)
  between operations  15.7 us (3%)
    all_gather x1, waiting for transfers between devices, on_device(): piece_keys = lax.all_gather(cache_keys[None], 'seq', axis=0, tiled=True)  112 us
    all_gather x1, waiting for transfers between devices, on_device(): lax.all_gather(fresh_values[None], 'seq', axis=0, tiled=True)  75.4 us
    all_gather x1, waiting for transfers between devices, on_device(): piece_values = lax.all_gather(cache_values[None], 'seq', axis=0, tiled=True)  70.7 us
    all_gather x1, waiting for transfers between devices, on_device(): piece = lax.all_gather(hidden, 'tp', axis=1, tiled=True)  58.6 us
    reduce_scatter x1, waiting for transfers between devices, on_device(): lax.psum_scatter(partial_out.astype(jnp.bfloat16), 'tp', scatter_dimensio...  52.6 us
    dot_general x2, matrix products, attend(): jnp.einsum('krn,nkd->krd', weights.astype(jnp.bfloat16), values, preferre...  40.8 us
    dot_general x2, matrix products, attend(): jnp.einsum('krd,nkd->krn', grouped, keys, preferred_element_type=jnp.floa...  34.3 us
    reduce_sum x2, other arithmetic, attend(): total = total * rescale + jnp.sum(weights, axis=-1)  29.7 us
  transfers between devices with their start and end apart: 6, of which 6 were waited for; matrix products, arithmetic and copies ran while one was open for 18% of the time, Pallas kernels for 0%

commit v1 on v0

--- a/solution.py
+++ b/solution.py
@@ -9,6 +9,18 @@
 CTX = 2048
 ROPE_BASE = 1000000.0
 masked_score = -1e30
+
+
+def gather_by_bits(value, axis, dim):
+    ways, here, step = (lax.axis_size(axis), lax.axis_index(axis), value.shape[dim])
+    line, have = (value, 1)
+    while have < ways:
+        line = jnp.concatenate(
+            [line, lax.ppermute(line, axis, [(d, (d - have) % ways) for d in range(ways)])],
+            axis=dim,
+        )
+        have = 2 * have
+    return jnp.roll(line, here * step, axis=dim)
 
 
 def norm_rope(values, positions):
@@ -99,7 +111,7 @@
         jnp.zeros((kv_heads, group * tokens_here, HD), jnp.float32),
     )
     carry = state
-    piece_keys = lax.all_gather(cache_keys[None], "seq", axis=0, tiled=True)
+    piece_keys = gather_by_bits(cache_keys[None], "seq", 0)
     piece_values = lax.all_gather(cache_values[None], "seq", axis=0, tiled=True)
     piece_table = lax.all_gather(page_table[None], "seq", axis=0, tiled=True)
     piece_fresh_k = lax.all_gather(fresh_keys[None], "seq", axis=0, tiled=True)

time: 622 us -> 1060 us (1.70)
  waiting for transfers between devices: 383 us -> 652 us
  blocking collectives: 21.8 us -> 121 us
  local copies, waits for them, and re-layouts: 37.4 us -> 89.3 us
    ppermute x0 -> x4, waiting for transfers between devices: none -> 539 us  [gather_by_bits(): lax.ppermute(line, axis, [(d, (d - have) % ways) for d in range(ways)])]
    all_gather x1 -> x0, waiting for transfers between devices: 112 us -> none  [on_device(): piece_keys = lax.all_gather(cache_keys[None], 'seq', axis=0, tiled=True)]
    all_gather x1, blocking collectives: 21.8 us -> 121 us  [on_device(): piece_table = lax.all_gather(page_table[None], 'seq', axis=0, tiled=True)]
    all_gather x1, waiting for transfers between devices: 75.4 us -> 0.02 us  [on_device(): lax.all_gather(fresh_values[None], 'seq', axis=0, tiled=True)]
    all_gather x1, waiting for transfers between devices: 70.7 us -> 0.01 us  [on_device(): piece_values = lax.all_gather(cache_values[None], 'seq', axis=0, tiled=True)]
    unnamed x12 -> x35, local copies, waits for them, and re-layouts: 7.19 us -> 35.3 us
    dynamic_slice x0 -> x1, local copies, waits for them, and re-layouts: none -> 14 us  [gather_by_bits(): return jnp.roll(line, here * step, axis=dim)]
    all_gather x1, waiting for transfers between devices: 11.7 us -> 0.02 us  [on_device(): piece_fresh_k = lax.all_gather(fresh_keys[None], 'seq', axis=0, tiled=True)]
  transfers between devices with their start and end apart: 6 -> 9, of which waited for: 6 -> 5; matrix products, arithmetic and copies ran while one was open for 18% -> 18% of each run, Pallas kernels for 0% -> 0%
where the time goes in v1:
time: 1060 us; the launch traced here: 1050 us
  waiting for transfers between devices  652 us (62%)
  blocking collectives  121 us (11%)
  matrix products  109 us (10%)
  local copies, waits for them, and re-layouts  89.3 us (8%)
  other arithmetic  54.2 us (5%)
  between operations  15.6 us (1%)
    ppermute x4, waiting for transfers between devices, gather_by_bits(): lax.ppermute(line, axis, [(d, (d - have) % ways) for d in range(ways)])  539 us
    all_gather x1, blocking collectives, on_device(): piece_table = lax.all_gather(page_table[None], 'seq', axis=0, tiled=True)  121 us
    all_gather x1, waiting for transfers between devices, on_device(): piece = lax.all_gather(hidden, 'tp', axis=1, tiled=True)  58.6 us
    reduce_scatter x1, waiting for transfers between devices, on_device(): lax.psum_scatter(partial_out.astype(jnp.bfloat16), 'tp', scatter_dimensio...  53.4 us
    dot_general x2, matrix products, attend(): jnp.einsum('krn,nkd->krd', weights.astype(jnp.bfloat16), values, preferre...  40.5 us
    unnamed x35, local copies, waits for them, and re-layouts  35.3 us
    dot_general x2, matrix products, attend(): jnp.einsum('krd,nkd->krn', grouped, keys, preferred_element_type=jnp.floa...  29.6 us
    reduce_sum x2, other arithmetic, attend(): total = total * rescale + jnp.sum(weights, axis=-1)  25.8 us
  transfers between devices with their start and end apart: 9, of which 5 were waited for; matrix products, arithmetic and copies ran while one was open for 18% of the time, Pallas kernels for 0%

profile of v1, /device:TPU:0, one launch (start us, length us, event | category | flops | bytes accessed | tf_op | source)
XLA Modules:
  0.0 1049.5 jit_solution(10125449172548144068)
XLA Ops:
  9.8 58.6 %all-gather.9.cloned.1.call-done = bf16[512,4096]{1,0:T(8,128)(2,1)} async-done(((bf16[512,2048]{1,0:T(8,128)(2,1)}), bf16[512,4096]{1,0:T(8,128)(2,1)}) %all-gather.9.cloned.1.call-update) | async-done | bytes 4194320 | tf_op jit(solution)/shard_map/all_gather | solution.py:67
  68.4 5.9 multiply_reduce_fusion.1
  75.7 6.7 convolution_convert_fusion.1
  86.2 26.5 %collective-permute-done = bf16[1,16,64,512]{3,2,1,0:T(8,128)(2,1)S(1)} collective-permute-done((bf16[1,16,64,512]{3,2,1,0:T(8,128)(2,1)S(1)}, bf16[1,16,64,512]{3,2,1,0:T(8,128)(2,1)S(1)}, u32[]{:S(2)}, u32[]{:S(2)}) %collective-permute-start) | collective-permute-done | bytes 1048608 | tf_op jit(solution)/shard_map/ppermute | solution.py:19
  114.0 76.0 %collective-permute-done.1 = bf16[2,16,64,512]{3,2,1,0:T(8,128)(2,1)S(1)} collective-permute-done((bf16[2,16,64,512]{3,2,1,0:T(8,128)(2,1)S(1)}, bf16[2,16,64,512]{3,2,1,0:T(8,128)(2,1)S(1)}, u32[]{:S(2)}, u32[]{:S(2)}) %collective-permute-start.1) | collective-permute-done | bytes 2097184 | tf_op jit(solution)/shard_map/ppermute | solution.py:19
  193.2 4.5 collective-permute-start.2
  198.7 121.1 %all-gather.3 = s32[16,16,2]{1,2,0:T(2,128)S(1)} all-gather(s32[1,16,2]{1,2,0:T(2,128)S(1)} %bitcast.69), channel_id=2, replica_groups=mesh['seq'=16,'tp'=2] {'seq'}, dimensions={0}, use_global_device_ids=true | all-gather | bytes 2176 | tf_op jit(solution)/shard_map/all_gather | solution.py:116
  321.2 6.8 pad_maximum_fusion
  341.2 11.7 %convolution_bitcast_fusion = f32[64,8,16,128]{3,1,2,0:T(8,128)S(1)} fusion(bf16[512,4096]{1,0:T(8,128)(2,1)S(1)} %copy-done.10, bf16[4096,2048]{1,0:T(8,128)(2,1)} %param.10), kind=kOutput, calls=%fused_computation.26 | convolution fusion | flops 8589934592 | bytes 25165824 | tf_op jit(solution)/shard_map/dot_general | solution.py:70
  368.8 4.8 constant_dynamic-update-slice_fusion.6
  373.6 436.5 %collective-permute-done.3 = bf16[8,16,64,512]{3,2,1,0:T(8,128)(2,1)} collective-permute-done((bf16[8,16,64,512]{3,2,1,0:T(8,128)(2,1)}, bf16[8,16,64,512]{3,2,1,0:T(8,128)(2,1)}, u32[]{:S(2)}, u32[]{:S(2)}) %collective-permute-start.3) | collective-permute-done | bytes 8388640 | tf_op jit(solution)/shard_map/ppermute | solution.py:19
  810.1 7.7 constant_dynamic-update-slice_fusion.5
  821.5 4.7 constant_dynamic-update-slice_fusion.1
  826.2 7.7 constant_dynamic-update-slice_fusion
  833.9 14.0 %constant_dynamic-slice_fusion.2 = bf16[16,16,64,512]{3,2,1,0:T(8,128)(2,1)} fusion(bf16[32,16,64,512]{3,2,1,0:T(8,128)(2,1)} %constant_dynamic-update-slice_fusion, s32[]{:T(128)S(6)} %select_n.104), kind=kLoop, calls=%fused_computation.83 | loop fusion | bytes 33554436 | tf_op jit(solution)/shard_map/jit(_roll_dynamic)/dynamic_slice | solution.py:23
  847.9 7.9 gather_fusion.1
  859.9 25.0 %fusion = (f32[4,2048]{1,0:T(4,128)S(1)}, f32[4,2048,2048]{1,2,0:T(8,128)}) fusion(pred[2048]{0:T(1024)(128)(4,1)S(1)} %and.113, bf16[4,2048,128]{2,1,0:T(8,128)(2,1)S(1)} %bitcast.58, bf16[2048,4,128]{2,1,0:T(4,128)(2,1)} %reshape_reshape.12), kind=kOutput, calls=%fused_computation.5 | convolution fusion | flops 4345290752 | bytes 71337984 | tf_op jit(solution)/shard_map/krd,nkd->krn/dot_general | solution.py:94
  891.4 4.6 fusion.6
  901.8 21.6 %fusion.1 = f32[4,2048]{1,0:T(4,128)S(1)} fusion(f32[4,2048,2048]{1,2,0:T(8,128)} %get-tuple-element.43, f32[4,2048]{1,0:T(4,128)S(1)} %get-tuple-element.35, pred[2048]{0:T(1024)(128)(4,1)S(1)} %and.113), kind=kLoop, calls=%fused_computation.6 | loop fusion | flops 83877888 | bytes 67176448 | tf_op jit(solution)/shard_map/reduce_sum | solution.py:102
  923.4 10.5 %fusion.9 = f32[4,2048,128]{2,1,0:T(8,128)} fusion(bf16[512,4,128]{0,2,1:T(8,128)(2,1)S(1)} %bitcast.66, f32[4,2048,512]{1,2,0:T(8,128)} %copy-done, f32[4,2048]{1,0:T(4,128)S(1)} %get-tuple-element.34, pred[2048,512]{0,1:T(8,128)(4,1)S(1)} %copy-done.6), kind=kOutput, calls=%fused_computation.16 | convolution fusion | flops 1094713344 | bytes 22577152 | tf_op jit(solution)/shard_map/krn,nkd->krd/dot_general | solution.py:103
  934.0 6.4 gather_fusion.2
  942.5 29.9 %divide_convert_fusion = bf16[4,2048,128]{2,1,0:T(8,128)(2,1)S(1)} fusion(f32[4,2048,128]{2,1,0:T(8,128)} %fusion.9, f32[4,2048,2048]{1,2,0:T(8,128)} %get-tuple-element.43, f32[4,2048]{1,0:T(4,128)S(1)} %get-tuple-element.35, pred[2048]{0:T(1024)(128)(4,1)S(1)} %and.113, bf16[2048,4,128]{2,1,0:T(4,128)(2,1)} %reshape_reshape.13, ...), kind=kOutput, calls=%fused_computation.20 | convolution fusion | flops 4384096256 | bytes 75630592 | tf_op jit(solution)/shard_map/krn,nkd->krd/dot_general | solution.py:103
  974.7 14.5 %convolution_convert_fusion = bf16[512,4096]{1,0:T(8,128)(2,1)} fusion(bf16[512,2048]{0,1:T(8,128)(2,1)} %bitcast.64, bf16[2048,4096]{1,0:T(8,128)(2,1)} %param.13), kind=kOutput, calls=%fused_computation.18 | convolution fusion | flops 8592031744 | bytes 23068672 | tf_op jit(solution)/shard_map/dot_general | solution.py:156
  989.3 53.4 %reduce-scatter.2.cloned.1.call-done = bf16[512,2048]{1,0:T(8,128)(2,1)} async-done(((bf16[512,4096]{1,0:T(8,128)(2,1)}), bf16[512,2048]{1,0:T(8,128)(2,1)}) %reduce-scatter.2.cloned.1.call-update) | async-done | bytes 2097168 | tf_op jit(solution)/shard_map/reduce_scatter | solution.py:157
  (102 shorter events, 66.9 us)
Async XLA Ops:
  6.5 61.8 %all-gather.9.cloned.1.call-start = ((), (), s32[]{:S(2)}) async-start(), calls=%async_computation.1 | async-start | bytes 6291456 | tf_op jit(solution)/shard_map/all_gather | solution.py:67
  7.3 877.7 %all-gather.11.cloned.1.call-start = ((), (), s32[]{:S(2)}) async-start(), calls=%async_computation.2 | async-start | bytes 8912896 | tf_op jit(solution)/shard_map/all_gather | solution.py:117
  75.6 6.8 copy-start.2
  75.6 809.3 %all-gather.15.cloned.1.call-start = ((), (), s32[]{:S(2)}) async-start(), calls=%async_computation.5 | async-start | bytes 8912896 | tf_op jit(solution)/shard_map/all_gather | solution.py:118
  82.4 851.6 %all-gather.13.cloned.1.call-start = ((), (), s32[]{:S(2)}) async-start(), calls=%async_computation.4 | async-start | bytes 17825792 | tf_op jit(solution)/shard_map/all_gather | solution.py:115
  82.4 30.3 %collective-permute-start = (bf16[1,16,64,512]{3,2,1,0:T(8,128)(2,1)S(1)}, bf16[1,16,64,512]{3,2,1,0:T(8,128)(2,1)S(1)}, u32[]{:S(2)}, u32[]{:S(2)}) collective-permute-start(bf16[1,16,64,512]{3,2,1,0:T(8,128)(2,1)S(1)} %bitcast.53), channel_id=1, source_target_pairs={{0,30},{2,0},{4,2},{6,4},{8,6},{10,8},{12,10},{14,12},{16,14},{18,... | collective-permute-start | bytes 3145736 | tf_op jit(solution)/shard_map/ppermute | solution.py:19
  86.2 956.5 %reduce-scatter.2.cloned.1.call-start = ((), (), s32[]{:S(2)}) async-start(), calls=%async_computation.3 | async-start | bytes 6291456 | tf_op jit(solution)/shard_map/reduce_scatter | solution.py:157
  112.8 1.0 copy-start.3
  113.9 84.8 %copy-start.9 = (s32[16,2]{0,1:T(2,128)S(1)}, s32[16,2]{0,1:T(2,128)}, u32[]{:S(2)}) copy-start(s32[16,2]{0,1:T(2,128)} %param.17) | copy-start | bytes 388
  113.9 76.1 %collective-permute-start.1 = (bf16[2,16,64,512]{3,2,1,0:T(8,128)(2,1)S(1)}, bf16[2,16,64,512]{3,2,1,0:T(8,128)(2,1)S(1)}, u32[]{:S(2)}, u32[]{:S(2)}) collective-permute-start(bf16[2,16,64,512]{3,2,1,0:T(8,128)(2,1)S(1)} %pad_maximum_fusion.3), channel_id=1, source_target_pairs={{0,28},{2,30},{4,0},{6,2},{8,4},{10,6},{12,8},{14,10},{16,12},{18,... | collective-permute-start | bytes 6291464 | tf_op jit(solution)/shard_map/ppermute | solution.py:19
  193.2 128.0 %collective-permute-start.2 = (bf16[4,16,64,512]{3,2,1,0:T(8,128)(2,1)}, bf16[4,16,64,512]{3,2,1,0:T(8,128)(2,1)}, u32[]{:S(2)}, u32[]{:S(2)}) collective-permute-start(bf16[4,16,64,512]{3,2,1,0:T(8,128)(2,1)} %pad_maximum_fusion.1), channel_id=1, source_target_pairs={{0,24},{2,26},{4,28},{6,30},{8,0},{10,2},{12,4},{14,6},{16,8},{18,... | collective-permute-start | bytes 12582920 | tf_op jit(solution)/shard_map/ppermute | solution.py:19
  328.0 482.1 %collective-permute-start.3 = (bf16[8,16,64,512]{3,2,1,0:T(8,128)(2,1)}, bf16[8,16,64,512]{3,2,1,0:T(8,128)(2,1)}, u32[]{:S(2)}, u32[]{:S(2)}) collective-permute-start(bf16[8,16,64,512]{3,2,1,0:T(8,128)(2,1)} %pad_maximum_fusion), channel_id=1, source_target_pairs={{0,16},{2,18},{4,20},{6,22},{8,24},{10,26},{12,28},{14,30},{16,0},... | collective-permute-start | bytes 25165832 | tf_op jit(solution)/shard_map/ppermute | solution.py:19
  334.9 6.4 copy-start.10
  353.9 2.0 copy-start.1
  359.6 4.1 copy-start.7
  373.6 445.3 %copy-start.4 = (bf16[1,16,64,512]{3,2,1,0:T(8,128)(2,1)S(1)}, bf16[1,16,64,512]{3,2,1,0:T(8,128)(2,1)}, u32[]{:S(2)}) copy-start(bf16[1,16,64,512]{3,2,1,0:T(8,128)(2,1)} %copy-done.3) | copy-start | bytes 3145732
  847.9 12.0 %copy-start.5 = (bf16[512,4,4,128]{3,0,2,1:T(8,128)(2,1)S(1)}, bf16[512,4,4,128]{3,0,2,1:T(8,128)(2,1)}, u32[]{:S(2)}) copy-start(bf16[512,4,4,128]{3,0,2,1:T(8,128)(2,1)} %pad_maximum_fusion.2) | copy-start | bytes 6291460
  884.9 6.5 copy-start.6
  896.0 5.8 copy-start
  901.8 21.6 %copy-start.8 = (bf16[1,512,512]{1,2,0:T(8,128)(2,1)S(1)}, bf16[1,512,512]{1,2,0:T(8,128)(2,1)}, u32[]{:S(2)}) copy-start(bf16[1,512,512]{1,2,0:T(8,128)(2,1)} %copy.99) | copy-start | bytes 1572868
Sparse Core Ops, SparseCore 0:
  8.9 59.4 all-gather.8
  75.8 113.8 all-gather.10
  191.8 347.2 all-gather.14
  541.2 175.5 all-gather.12
  989.4 53.2 reduce-scatter.1
